TPU v7x, 32 devices: a whole 2x2x4 slice. The times are simulated.
32 devices in a mesh: seq: 16 (over z, x, core), head: 2 (over y).
Axes of the slice: x: 2, y: 2, z: 4, core: 2. Of those that a mesh axis runs over, the one named last changes fastest.
Arguments:
- features: bfloat16 [8, 32, 8, 512], P(None, 'seq', 'head'), may hold values from -540 to 540
- gn_gain: float32 [512], replicated, may hold values from 0.5 to 1.5
- gn_bias: float32 [512], replicated, may hold values from -3 to 3
- conv_weight: bfloat16 [3, 3, 3, 16, 512], replicated, may hold values from -0.0546875 to 0.0546875
- conv_bias: float32 [16], replicated, may hold values from -3 to 3
- patch_weight: bfloat16 [64, 3072], replicated, may hold values from -0.75 to 0.75
- patch_bias: float32 [3072], replicated, may hold values from -3 to 3
- image_mod: float32 [3, 3072], replicated, may hold values from -3 to 3
- w_qkv: bfloat16 [3072, 3, 2048], P('seq', None, 'head'), may hold values from -5 to 5
- text_ids: int32 [512], replicated, may hold values from 0 to 16383
- text_length: int32 [1], replicated, may hold values from 256 to 512
- text_table: bfloat16 [3072, 16384], P('seq'), may hold values from -60 to 60
- text_mod: float32 [2, 3072], P(None, 'seq'), may hold values from -3 to 3
- w_text: bfloat16 [3072, 2, 2048], P('seq', None, 'head'), may hold values from -2 to 2
- w_out: bfloat16 [2048, 3072], P('head'), may hold values from -0.625 to 0.625
- out_bias: float32 [3072], replicated, may hold values from -3 to 3
Outputs:
- block_out: bfloat16 [8, 16, 4, 3072], P(None, 'seq', 'head')
All inputs are finite; a program needn't handle non-finite values.
Results may differ from a plain program's by a relative error of at most 0.0089.
Values may be sent and summed in bfloat16 or wider, within the bound.
A program may use at most 128 MiB of HBM per device.

v0:
```python
import math
import jax
import jax.numpy as jnp
from jax import lax
from jax.sharding import PartitionSpec as P

HD = 128
GN_GROUPS = 32
eps_norm = 1e-06


def with_halo(cells, sides, width):
    for axis, dim in sides:
        count = lax.axis_size(axis)
        ends = count - 1
        head = lax.slice_in_dim(cells, 0, width, axis=dim)
        tail = lax.slice_in_dim(cells, cells.shape[dim] - width, cells.shape[dim], axis=dim)
        cells = jnp.concatenate(
            [
                lax.ppermute(tail, axis, [(i, (i + 1) % count) for i in range(ends)]),
                cells,
                lax.ppermute(head, axis, [((i + 1) % count, i) for i in range(ends)]),
            ],
            axis=dim,
        )
    return cells


def patchify(latent):
    frame_count, row_count, col_count, chan_count = latent.shape
    blocks = latent.reshape(frame_count, row_count // 2, 2, col_count // 2, 2, chan_count)
    blocks = blocks.transpose(0, 1, 3, 2, 4, 5)
    return blocks.reshape(frame_count * (row_count // 2) * (col_count // 2), 4 * chan_count)


def embed_tokens(patches, patch_weight, patch_bias, image_mod):
    hidden = jnp.dot(patches, patch_weight, preferred_element_type=jnp.float32) + patch_bias
    center = jnp.mean(hidden, axis=1, keepdims=True)
    offset = hidden - center
    spread = jnp.mean(offset * offset, axis=1, keepdims=True)
    normed = offset * lax.rsqrt(spread + eps_norm)
    modulated = (normed * (1.0 + image_mod[1]) + image_mod[0]).astype(jnp.bfloat16)
    return (hidden, modulated)


def text_start(query, text_keys, text_values, text_valid):
    scores = jnp.einsum("qhe,khe->qhk", query, text_keys, preferred_element_type=jnp.float32) / HD
    scores = jnp.where(text_valid[None, None, :], scores, -1e30)
    first_top = jnp.max(scores, axis=2)
    probs = jnp.exp(scores - first_top[..., None])
    first_total = jnp.sum(probs, axis=2)
    first_acc = jnp.einsum(
        "qhk,khe->qhe", probs.astype(jnp.bfloat16), text_values, preferred_element_type=jnp.float32
    )
    return (first_top, first_total, first_acc)


def attend_rows(query, state, piece):
    piece_rows = piece.shape[0]
    block_rows = math.gcd(piece_rows, 2048)
    heads_count = query.shape[1]
    blocks = piece.reshape(piece_rows // block_rows, block_rows, 2, heads_count, HD)

    def one_block(inner, block):
        run_top, run_total, run_acc = inner
        scores = (
            jnp.einsum("qhe,khe->qhk", query, block[:, 0], preferred_element_type=jnp.float32) / HD
        )
        new_top = jnp.maximum(run_top, jnp.max(scores, axis=2))
        factor = jnp.exp(run_top - new_top)
        probs = jnp.exp(scores - new_top[..., None])
        run_total = run_total * factor + jnp.sum(probs, axis=2)
        run_acc = run_acc * factor[..., None] + jnp.einsum(
            "qhk,khe->qhe",
            probs.astype(jnp.bfloat16),
            block[:, 1],
            preferred_element_type=jnp.float32,
        )
        return ((new_top, run_total, run_acc), None)

    return lax.scan(one_block, state, blocks)[0]


def body(
    features,
    gn_gain,
    gn_bias,
    conv_weight,
    conv_bias,
    patch_weight,
    patch_bias,
    image_mod,
    w_qkv,
    text_ids,
    text_length,
    text_table,
    text_mod,
    w_text,
    w_out,
    out_bias,
):
    frame_count, row_count, col_count, chan_count = features.shape
    width_full = patch_weight.shape[1]
    values = features.astype(jnp.float32)
    grouped = values.reshape(frame_count, row_count, col_count, GN_GROUPS, chan_count // GN_GROUPS)
    group_sums = jnp.sum(grouped, axis=(0, 1, 2, 4))
    group_squares = jnp.sum(grouped * grouped, axis=(0, 1, 2, 4))
    group_sums, group_squares = lax.psum((group_sums, group_squares), ("seq", "head"))
    cell_count = (
        frame_count
        * row_count
        * col_count
        * (chan_count // GN_GROUPS)
        * lax.axis_size("seq")
        * lax.axis_size("head")
    )
    group_mean = group_sums / cell_count
    group_scale = lax.rsqrt(group_squares / cell_count - group_mean * group_mean + eps_norm)
    normed = ((grouped - group_mean[:, None]) * group_scale[:, None]).reshape(
        frame_count, row_count, col_count, chan_count
    )
    activated = jax.nn.silu(normed * gn_gain + gn_bias).astype(jnp.bfloat16)
    rimmed = with_halo(activated, (("seq", 1), ("head", 2)), 1)
    padded = jnp.concatenate([rimmed[:1], rimmed[:1], rimmed], axis=0)
    windows = []
    for time_off in range(3):
        for row_off in range(3):
            for col_off in range(3):
                windows.append(
                    padded[
                        time_off : time_off + frame_count,
                        row_off : row_off + row_count,
                        col_off : col_off + col_count,
                    ]
                )
    stacked = jnp.stack(windows, axis=3)
    latent_chans = conv_weight.shape[3]
    kernels = conv_weight.reshape(27, latent_chans, chan_count)
    latent_sum = jnp.einsum("fyxkc,kzc->fyxz", stacked, kernels, preferred_element_type=jnp.float32)
    latent = (latent_sum + conv_bias).astype(jnp.bfloat16)
    patches = patchify(latent)
    hidden, own_modulated = embed_tokens(patches, patch_weight, patch_bias, image_mod)
    modulated = lax.all_gather(own_modulated, "head", axis=0, tiled=True)
    token_count = modulated.shape[0]
    head_width = w_qkv.shape[2]
    heads_here = head_width // HD
    qkv = jnp.einsum(
        "nd,dkj->nkj",
        modulated,
        lax.all_gather(w_qkv, "seq", axis=0, tiled=True),
        preferred_element_type=jnp.float32,
    ).astype(jnp.bfloat16)
    context = jnp.take(text_table, text_ids, axis=1).astype(jnp.float32)
    text_weight = w_text.astype(jnp.float32)
    text_gain = 1.0 + text_mod[1]
    text_shift = text_mod[0]
    text_sums, text_squares = lax.psum(
        (jnp.sum(context, axis=0), jnp.sum(context * context, axis=0)), "seq"
    )
    text_mean = text_sums / width_full
    text_scale = lax.rsqrt(text_squares / width_full - text_mean * text_mean + eps_norm)
    text_normed = (context - text_mean) * text_scale * text_gain[:, None] + text_shift[:, None]
    partial_kv = jnp.einsum(
        "dt,dkj->tkj", text_normed, text_weight, precision=lax.Precision.HIGHEST
    )
    text_kv = lax.psum(partial_kv, "seq")
    text_kv = text_kv.astype(jnp.bfloat16)
    text_count = text_kv.shape[0]
    text_valid = jnp.arange(text_count, dtype=jnp.int32) < text_length[0]
    query = qkv[:, 0].reshape(token_count, heads_here, HD)
    text_keys = text_kv[:, 0].reshape(text_count, heads_here, HD)
    text_values = text_kv[:, 1].reshape(text_count, heads_here, HD)
    first_state = text_start(query, text_keys, text_values, text_valid)
    image_kv = qkv[:, 1:3]
    run_top, run_total, run_acc = attend_rows(
        query, first_state, lax.all_gather(image_kv, "seq", axis=0, tiled=True)
    )
    attended = (
        (run_acc / run_total[..., None]).astype(jnp.bfloat16).reshape(token_count, head_width)
    )
    projected = (
        lax.psum_scatter(
            jnp.dot(attended, w_out, preferred_element_type=jnp.float32),
            "head",
            scatter_dimension=0,
            tiled=True,
        )
        + out_bias
    )
    block_out = (hidden + image_mod[2] * projected).astype(jnp.bfloat16)
    return block_out.reshape(frame_count, row_count // 2, col_count // 2, width_full)


def solution(mesh):
    return jax.shard_map(
        body,
        mesh=mesh,
        in_specs=(
            P(None, "seq", "head", None),
            P(),
            P(),
            P(),
            P(),
            P(),
            P(),
            P(),
            P("seq", None, "head"),
            P(),
            P(),
            P("seq", None),
            P(None, "seq"),
            P("seq", None, "head"),
            P("head", None),
            P(),
        ),
        out_specs=P(None, "seq", "head", None),
        check_vma=False,
    )
```

profile of v0, /device:TPU:0, one launch (start us, length us, event | category | flops | bytes accessed | tf_op | source)
XLA Modules:
  0.0 285.2 jit_solution(11076966553390359524)
XLA Ops:
  6.5 0.7 all-gather.3.cloned.1.call-update
  7.3 0.9 convert_reduce_fusion.1
  8.6 43.1 %all-reduce = (f32[32]{0:T(128)S(1)}, f32[32]{0:T(128)S(1)}) all-reduce(f32[32]{0:T(128)S(1)} %reduce_sum.92, f32[32]{0:T(128)S(1)} %reduce_sum.89), channel_id=1, replica_groups=mesh['seq'=16,'head'=2] {'seq','head'}, use_global_device_ids=true, to_apply=%region_5.6 | all-reduce | flops 64 | bytes 512 | tf_op jit(solution)/shard_map/psum | solution.py:108
  52.0 1.0 fusion.41
  52.9 1.8 collective-permute-start
  54.7 1.3 collective-permute-start.1
  56.0 0.7 compare_select_fusion
  56.7 1.0 fusion.78
  57.7 0.7 compare_and_fusion
  58.4 1.5 collective-permute-done.1
  59.9 2.5 collective-permute-start.2
  62.4 1.3 collective-permute-start.3
  63.7 10.1 %copy.82 = bf16[192,16384]{0,1:T(8,128)(2,1)} copy(bf16[192,16384]{1,0:T(8,128)(2,1)} %param.27) | data formatting | bytes 12582912 | tf_op args[11]
  73.8 6.2 %gather_fusion = bf16[512,192]{1,0:T(8,128)(2,1)S(1)} fusion(bf16[192,16384]{0,1:T(8,128)(2,1)} %copy.82, s32[1024]{0:T(1024)S(1)} %pad_clamp_fusion), kind=kCustom, calls=%fused_computation | custom fusion | bytes 395264 | tf_op jit(solution)/shard_map/jit(_take)/gather | solution.py:153
  81.6 0.6 fusion.9
  82.9 5.9 %all_gather.9 = bf16[32,3072]{1,0:T(8,128)(2,1)S(1)} all-gather(bf16[16,3072]{1,0:T(8,128)(2,1)S(1)} %add_convert_fusion.1), channel_id=1, replica_groups=mesh['seq'=16,'head'=2] {'head'}, dimensions={0}, use_global_device_ids=true | all-gather | bytes 294912 | tf_op jit(solution)/shard_map/all_gather | solution.py:143
  88.8 23.2 %all-gather.3.cloned.1.call-done = bf16[3072,3,1024]{2,0,1:T(8,128)(2,1)} async-done(((bf16[192,3,1024]{2,0,1:T(8,128)(2,1)}), bf16[3072,3,1024]{2,0,1:T(8,128)(2,1)}) %all-gather.3.cloned.1.call-update) | async-done | bytes 18874384 | tf_op jit(solution)/shard_map/all_gather | solution.py:150
  112.0 9.7 %convolution_convert_fusion = bf16[32,3,1024]{2,0,1:T(8,128)(2,1)S(1)} fusion(bf16[3072,3,1024]{2,0,1:T(8,128)(2,1)} %all-gather.3.cloned.1.call-done, bf16[32,3072]{1,0:T(8,128)(2,1)S(1)} %all_gather.9), kind=kOutput, calls=%fused_computation.7 | convolution fusion | flops 604078080 | bytes 19267584 | tf_op jit(solution)/shard_map/nd,dkj->nkj/dot_general | solution.py:147
  121.7 0.7 slice.219
  122.8 33.0 %all-reduce.1 = (f32[512]{0:T(512)S(1)}, f32[512]{0:T(512)S(1)}) all-reduce(f32[512]{0:T(512)S(1)} %get-tuple-element.16, f32[512]{0:T(512)S(1)} %get-tuple-element.15), channel_id=1, replica_groups=mesh['seq'=16,'head'=2] {'seq'}, use_global_device_ids=true, to_apply=%region_9.10 | all-reduce | flops 1024 | bytes 8192 | tf_op jit(solution)/shard_map/psum | solution.py:157
  155.8 3.9 %fusion.12 = f32[512,2,1024]{2,0,1:T(8,128)} fusion(bf16[192,2,1024]{2,1,0:T(2,128)(2,1)S(1)} %copy-done, f32[192]{0:T(256)S(1)} %bitcast.263, f32[192]{0:T(256)S(1)} %bitcast.262, f32[512]{0:T(512)S(1)} %get-tuple-element.47, f32[512]{0:T(512)S(1)} %get-tuple-element.46, bf16[512,192]{1,0:T(8,128)(2,1)S(1)} %gather_fusion, ...), kind=kOutput, calls=%fused_computation.24 | convolution fusion | flops 2416508928 | bytes 5183488 | tf_op jit(solution)/shard_map/dt,dkj->tkj/dot_general | solution.py:163
  159.7 94.6 %all-reduce.3 = bf16[512,2,1024]{2,0,1:T(8,128)(2,1)S(1)} all-reduce(f32[512,2,1024]{2,0,1:T(8,128)} %fusion.12), channel_id=1, replica_groups=mesh['seq'=16,'head'=2] {'seq'}, use_global_device_ids=true, to_apply=%region_10.11 | all-reduce | flops 1048576 | bytes 6291456 | tf_op jit(solution)/shard_map/psum | solution.py:166
  255.8 1.3 fusion.80
  257.0 2.4 copy.103
  259.6 0.6 fusion.81
  260.1 0.6 copy-done.2
  261.1 0.4 convolution_bitcast_fusion
  261.5 0.4 fusion.7
  261.9 1.9 fusion.43
  263.9 13.2 %reduce-scatter.2.cloned.1.call-done = f32[16,3072]{1,0:T(8,128)} async-done(((f32[32,3072]{1,0:T(8,128)}), f32[16,3072]{1,0:T(8,128)}) %reduce-scatter.2.cloned.1.call-update) | async-done | bytes 196624 | tf_op jit(solution)/shard_map/reduce_scatter | solution.py:182
  277.1 1.0 add_convert_fusion
  278.0 0.7 reshape.87
  (98 shorter events, 4.4 us)
Async XLA Ops:
  6.5 149.3 %copy-start = (bf16[192,2,1024]{2,1,0:T(2,128)(2,1)S(1)}, bf16[192,2,1024]{2,1,0:T(2,128)(2,1)}, u32[]{:S(2)}) copy-start(bf16[192,2,1024]{2,1,0:T(2,128)(2,1)} %param.29) | copy-start | bytes 2359300
  6.5 105.4 %all-gather.3.cloned.1.call-start = ((), (), s32[]{:S(2)}) async-start(), calls=%async_computation.1 | async-start | bytes 20054016 | tf_op jit(solution)/shard_map/all_gather | solution.py:150
  7.3 249.8 %all-gather.5.cloned.1.call-start = ((), (), s32[]{:S(2)}) async-start(), calls=%async_computation.2 | async-start | bytes 2228224 | tf_op jit(solution)/shard_map/all_gather | solution.py:176
  52.9 5.4 %collective-permute-start = (bf16[8,1,4,512]{3,0,2,1:T(8,128)(2,1)S(1)}, bf16[8,1,4,512]{3,0,2,1:T(8,128)(2,1)S(1)}, u32[]{:S(2)}, u32[]{:S(2)}) collective-permute-start(bf16[8,1,4,512]{3,0,2,1:T(8,128)(2,1)S(1)} %get-tuple-element.41), channel_id=1, source_target_pairs={{0,2},{2,4},{4,6},{6,8},{8,10},{10,12},{12,14},{14,16},{16,18},{18... | collective-permute-start | bytes 98312 | tf_op jit(solution)/shard_map/ppermute | solution.py:20
  54.7 5.2 %collective-permute-start.1 = (bf16[8,1,4,512]{3,0,2,1:T(8,128)(2,1)S(1)}, bf16[8,1,4,512]{3,0,2,1:T(8,128)(2,1)S(1)}, u32[]{:S(2)}, u32[]{:S(2)}) collective-permute-start(bf16[8,1,4,512]{3,0,2,1:T(8,128)(2,1)S(1)} %get-tuple-element.42), channel_id=1, source_target_pairs={{2,0},{4,2},{6,4},{8,6},{10,8},{12,10},{14,12},{16,14},{18,16},{20... | collective-permute-start | bytes 98312 | tf_op jit(solution)/shard_map/ppermute | solution.py:22
  59.9 20.1 %collective-permute-start.2 = (bf16[8,4,1,512]{3,0,2,1:T(8,128)(2,1)S(1)}, bf16[8,4,1,512]{3,0,2,1:T(8,128)(2,1)S(1)}, u32[]{:S(2)}, u32[]{:S(2)}) collective-permute-start(bf16[8,4,1,512]{3,0,2,1:T(8,128)(2,1)S(1)} %get-tuple-element.39), channel_id=1, source_target_pairs={{0,1},{2,3},{4,5},{6,7},{8,9},{10,11},{12,13},{14,15},{16,17},{18,... | collective-permute-start | bytes 98312 | tf_op jit(solution)/shard_map/ppermute | solution.py:20
  62.4 17.6 %collective-permute-start.3 = (bf16[8,4,1,512]{3,0,2,1:T(8,128)(2,1)S(1)}, bf16[8,4,1,512]{3,0,2,1:T(8,128)(2,1)S(1)}, u32[]{:S(2)}, u32[]{:S(2)}) collective-permute-start(bf16[8,4,1,512]{3,0,2,1:T(8,128)(2,1)S(1)} %get-tuple-element.40), channel_id=1, source_target_pairs={{1,0},{3,2},{5,4},{7,6},{9,8},{11,10},{13,12},{15,14},{17,16},{19,... | collective-permute-start | bytes 98312 | tf_op jit(solution)/shard_map/ppermute | solution.py:22
  80.3 0.8 copy-start.1
  80.4 0.8 copy-start.7
  80.4 0.8 copy-start.8
  80.5 1.0 copy-start.3
  80.5 1.0 copy-start.9
  80.8 1.5 copy-start.4
  80.8 1.5 copy-start.5
  88.8 67.0 %copy-start.10 = (f32[2,192]{1,0:T(2,128)S(1)}, f32[2,192]{1,0:T(2,128)}, u32[]{:S(2)}) copy-start(f32[2,192]{1,0:T(2,128)} %param.28) | copy-start | bytes 4612
  122.4 154.7 %reduce-scatter.2.cloned.1.call-start = ((), (), s32[]{:S(2)}) async-start(), calls=%async_computation.3 | async-start | bytes 589824 | tf_op jit(solution)/shard_map/reduce_scatter | solution.py:182
  257.0 4.9 %slice-start = ((s8[6291456]{0:T(1024)(128)(4,1)}), s8[4194304]{0:T(1024)(128)(4,1)S(1)}, s32[]{:S(2)}) async-start(s8[6291456]{0:T(1024)(128)(4,1)} %bitcast.249), calls=%async_computation.4 | async-start | bytes 8388608
  259.4 2.5 slice-start.1
  259.6 1.2 copy-start.2
  261.9 15.2 %copy-start.6 = (f32[3072]{0:T(1024)S(1)}, f32[3072]{0:T(1024)}, u32[]{:S(2)}) copy-start(f32[3072]{0:T(1024)} %param.31) | copy-start | bytes 36868
Sparse Core Ops, SparseCore 0:
  8.9 103.0 all-gather.2
  122.5 42.3 all-gather.4
  264.0 12.9 reduce-scatter.1
where the time goes:
time: 286 us; the launch traced here: 285 us
  blocking collectives  177 us (62%)
  waiting for transfers between devices  38.6 us (13%)
  local copies, waits for them, and re-layouts  22.7 us (8%)
  matrix products  19.1 us (7%)
  between operations  14.3 us (5%)
  starting transfers between devices  6.94 us (2%)
  other arithmetic  6.94 us (2%)
    psum x1, blocking collectives, body(): text_kv = lax.psum(partial_kv, 'seq')  94.6 us
    psum x1, blocking collectives, body(): lax.psum((group_sums, group_squares), ('seq', 'head'))  43.1 us
    psum x1, blocking collectives, body(): lax.psum((jnp.sum(context, axis=0), jnp.sum(context * context, axis=0)),...  33 us
    all_gather x1, waiting for transfers between devices, body(): lax.all_gather(w_qkv, 'seq', axis=0, tiled=True)  23.2 us
    unnamed x56, local copies, waits for them, and re-layouts  14.5 us
    reduce_scatter x1, waiting for transfers between devices, body(): lax.psum_scatter(jnp.dot(attended, w_out, preferred_element_type=jnp.floa...  13.2 us
    dot_general x1, matrix products, body(): jnp.einsum('nd,dkj->nkj', modulated, lax.all_gather(w_qkv, 'seq', axis=0,...  9.7 us
    gather x1, local copies, waits for them, and re-layouts, body(): context = jnp.take(text_table, text_ids, axis=1).astype(jnp.float32)  6.18 us
  transfers between devices with their start and end apart: 7, of which 3 were waited for; matrix products, arithmetic and copies ran while one was open for 10% of the time, Pallas kernels for 0%

commit v1 on v0

--- a/solution.py
+++ b/solution.py
@@ -3,10 +3,17 @@
 import jax.numpy as jnp
 from jax import lax
 from jax.sharding import PartitionSpec as P
+from jax.lax import psum
 
 HD = 128
 GN_GROUPS = 32
 eps_norm = 1e-06
+
+
+def arrange_the_tracks(my_data):
+    for k0 in ("head", "seq"):
+        my_data = psum(my_data, k0)
+    return my_data
 
 
 def with_halo(cells, sides, width):
@@ -105,7 +112,7 @@
     grouped = values.reshape(frame_count, row_count, col_count, GN_GROUPS, chan_count // GN_GROUPS)
     group_sums = jnp.sum(grouped, axis=(0, 1, 2, 4))
     group_squares = jnp.sum(grouped * grouped, axis=(0, 1, 2, 4))
-    group_sums, group_squares = lax.psum((group_sums, group_squares), ("seq", "head"))
+    group_sums, group_squares = arrange_the_tracks((group_sums, group_squares))
     cell_count = (
         frame_count
         * row_count

time: 286 us -> 306 us (1.070)
  waiting for transfers between devices: 38.6 us -> 57 us
  other arithmetic: 6.94 us -> 2.95 us
    all_gather x1, waiting for transfers between devices: 0.01 us -> 37.3 us  [body(): lax.all_gather(image_kv, 'seq', axis=0, tiled=True)]
    all_gather x1, waiting for transfers between devices: 23.2 us -> 0.01 us  [body(): lax.all_gather(w_qkv, 'seq', axis=0, tiled=True)]
    ppermute x2, waiting for transfers between devices: 1.55 us -> 6.64 us  [with_halo(): lax.ppermute(head, axis, [((i + 1) % count, i) for i in range(ends)])]
  transfers between devices with their start and end apart: 7 -> 7, of which waited for: 3 -> 5; matrix products, arithmetic and copies ran while one was open for 10% -> 9% of each run, Pallas kernels for 0% -> 0%
where the time goes in v1:
time: 306 us; the launch traced here: 305 us
  blocking collectives  179 us (58%)
  waiting for transfers between devices  57 us (19%)
  local copies, waits for them, and re-layouts  22.7 us (7%)
  matrix products  19.4 us (6%)
  between operations  14.4 us (5%)
  starting transfers between devices  10 us (3%)
    psum x2, blocking collectives, arrange_the_tracks(): my_data = psum(my_data, k0)  138 us
    all_gather x1, waiting for transfers between devices, body(): lax.all_gather(image_kv, 'seq', axis=0, tiled=True)  37.3 us
    psum x1, blocking collectives, body(): lax.psum((jnp.sum(context, axis=0), jnp.sum(context * context, axis=0)),...  35.2 us
    unnamed x56, local copies, waits for them, and re-layouts  13.8 us
    reduce_scatter x1, waiting for transfers between devices, body(): lax.psum_scatter(jnp.dot(attended, w_out, preferred_element_type=jnp.floa...  12 us
    dot_general x1, matrix products, body(): jnp.einsum('nd,dkj->nkj', modulated, lax.all_gather(w_qkv, 'seq', axis=0,...  9.7 us
    ppermute x2, starting transfers between devices, with_halo(): lax.ppermute(tail, axis, [(i, (i + 1) % count) for i in range(ends)])  7.19 us
    gather x1, local copies, waits for them, and re-layouts, body(): context = jnp.take(text_table, text_ids, axis=1).astype(jnp.float32)  6.8 us
  transfers between devices with their start and end apart: 7, of which 5 were waited for; matrix products, arithmetic and copies ran while one was open for 9% of the time, Pallas kernels for 0%

profile of v1, /device:TPU:0, one launch (start us, length us, event | category | flops | bytes accessed | tf_op | source)
XLA Modules:
  0.0 305.3 jit_solution(11119749072497073627)
XLA Ops:
  6.5 0.7 all-gather.3.cloned.1.call-update
  7.3 10.0 %copy.82 = bf16[192,16384]{0,1:T(8,128)(2,1)} copy(bf16[192,16384]{1,0:T(8,128)(2,1)} %param.27) | data formatting | bytes 12582912 | tf_op args[11]
  17.3 6.8 %gather_fusion = bf16[512,192]{1,0:T(8,128)(2,1)S(1)} fusion(bf16[192,16384]{0,1:T(8,128)(2,1)} %copy.82, s32[1024]{0:T(1024)S(1)} %pad_clamp_fusion), kind=kCustom, calls=%fused_computation | custom fusion | bytes 395264 | tf_op jit(solution)/shard_map/jit(_take)/gather | solution.py:160
  24.1 0.4 convert_reduce_fusion
  24.5 35.2 %all-reduce.1 = (f32[512]{0:T(512)S(1)}, f32[512]{0:T(512)S(1)}) all-reduce(f32[512]{0:T(512)S(1)} %get-tuple-element.16, f32[512]{0:T(512)S(1)} %get-tuple-element.15), channel_id=1, replica_groups=mesh['seq'=16,'head'=2] {'seq'}, use_global_device_ids=true, to_apply=%region_11.12 | all-reduce | flops 1024 | bytes 8192 | tf_op jit(solution)/shard_map/psum | solution.py:164
  59.7 4.0 %fusion.12 = f32[512,2,1024]{2,0,1:T(8,128)} fusion(bf16[192,2,1024]{2,1,0:T(2,128)(2,1)S(1)} %copy-done, f32[192]{0:T(256)S(1)} %bitcast.263, f32[192]{0:T(256)S(1)} %bitcast.262, f32[512]{0:T(512)S(1)} %get-tuple-element.50, f32[512]{0:T(512)S(1)} %get-tuple-element.49, bf16[512,192]{1,0:T(8,128)(2,1)S(1)} %gather_fusion, ...), kind=kOutput, calls=%fused_computation.24 | convolution fusion | flops 2416508928 | bytes 5183488 | tf_op jit(solution)/shard_map/dt,dkj->tkj/dot_general | solution.py:170
  64.1 4.9 %all-reduce.2 = (f32[32]{0:T(128)S(1)}, f32[32]{0:T(128)S(1)}) all-reduce(f32[32]{0:T(128)S(1)} %reduce_sum.92, f32[32]{0:T(128)S(1)} %reduce_sum.89), channel_id=1, replica_groups=mesh['seq'=16,'head'=2] {'head'}, use_global_device_ids=true, to_apply=%region_6.7 | all-reduce | flops 64 | bytes 512 | tf_op jit(solution)/shard_map/psum | solution.py:15
  69.1 132.7 %all-reduce.4 = (f32[32]{0:T(128)S(1)}, f32[32]{0:T(128)S(1)}, bf16[512,2,1024]{2,0,1:T(8,128)(2,1)S(1)}) all-reduce(f32[32]{0:T(128)S(1)} %get-tuple-element.32, f32[32]{0:T(128)S(1)} %get-tuple-element.33, f32[512,2,1024]{2,0,1:T(8,128)} %fusion.12), channel_id=1, replica_groups=mesh['seq'=16,'head'=2] {'seq'}, use_global_device_ids=true, to_apply=%region_7.8 | all-reduce | flops 1048640 | bytes 6291968 | tf_op jit(solution)/shard_map/psum | solution.py:15
  202.2 3.8 %collective-permute-start = (bf16[8,1,4,512]{3,0,2,1:T(8,128)(2,1)S(1)}, bf16[8,1,4,512]{3,0,2,1:T(8,128)(2,1)S(1)}, u32[]{:S(2)}, u32[]{:S(2)}) collective-permute-start(bf16[8,1,4,512]{3,0,2,1:T(8,128)(2,1)S(1)} %get-tuple-element.44), channel_id=1, source_target_pairs={{0,2},{2,4},{4,6},{6,8},{8,10},{10,12},{12,14},{14,16},{16,18},{18... | collective-permute-start | bytes 98312 | tf_op jit(solution)/shard_map/ppermute | solution.py:27
  206.0 1.3 collective-permute-start.1
  207.3 2.4 collective-permute-done.1
  209.8 3.4 %collective-permute-start.2 = (bf16[8,4,1,512]{3,0,2,1:T(8,128)(2,1)S(1)}, bf16[8,4,1,512]{3,0,2,1:T(8,128)(2,1)S(1)}, u32[]{:S(2)}, u32[]{:S(2)}) collective-permute-start(bf16[8,4,1,512]{3,0,2,1:T(8,128)(2,1)S(1)} %get-tuple-element.42), channel_id=1, source_target_pairs={{0,1},{2,3},{4,5},{6,7},{8,9},{10,11},{12,13},{14,15},{16,17},{18,... | collective-permute-start | bytes 98312 | tf_op jit(solution)/shard_map/ppermute | solution.py:27
  213.2 1.3 collective-permute-start.3
  214.8 4.2 %collective-permute-done.3 = bf16[8,4,1,512]{3,0,2,1:T(8,128)(2,1)S(1)} collective-permute-done((bf16[8,4,1,512]{3,0,2,1:T(8,128)(2,1)S(1)}, bf16[8,4,1,512]{3,0,2,1:T(8,128)(2,1)S(1)}, u32[]{:S(2)}, u32[]{:S(2)}) %collective-permute-start.3) | collective-permute-done | bytes 32800 | tf_op jit(solution)/shard_map/ppermute | solution.py:29
  219.9 0.5 copy-done.2
  220.5 0.6 fusion.9
  221.2 1.3 fusion.79
  222.8 6.1 %all_gather.9 = bf16[32,3072]{1,0:T(8,128)(2,1)S(1)} all-gather(bf16[16,3072]{1,0:T(8,128)(2,1)S(1)} %add_convert_fusion.1), channel_id=1, replica_groups=mesh['seq'=16,'head'=2] {'head'}, dimensions={0}, use_global_device_ids=true | all-gather | bytes 294912 | tf_op jit(solution)/shard_map/all_gather | solution.py:150
  228.9 9.7 %convolution_convert_fusion = bf16[32,3,1024]{2,0,1:T(8,128)(2,1)S(1)} fusion(bf16[3072,3,1024]{2,0,1:T(8,128)(2,1)} %all-gather.3.cloned.1.call-done, bf16[32,3072]{1,0:T(8,128)(2,1)S(1)} %all_gather.9), kind=kOutput, calls=%fused_computation.7 | convolution fusion | flops 604078080 | bytes 19267584 | tf_op jit(solution)/shard_map/nd,dkj->nkj/dot_general | solution.py:154
  238.6 0.7 slice.219
  239.7 0.3 copy.100
  241.0 0.6 fusion.80
  241.6 37.3 %all-gather.5.cloned.1.call-done = bf16[512,2,1024]{2,0,1:T(8,128)(2,1)} async-done(((bf16[32,2,1024]{2,0,1:T(8,128)(2,1)}), bf16[512,2,1024]{2,0,1:T(8,128)(2,1)}) %all-gather.5.cloned.1.call-update) | async-done | bytes 2097168 | tf_op jit(solution)/shard_map/all_gather | solution.py:183
  278.9 2.4 copy.103
  281.4 0.6 fusion.81
  282.0 0.3 fusion.20
  282.3 0.4 convolution_bitcast_fusion
  282.7 0.4 fusion.7
  283.2 1.9 fusion.43
  285.1 12.0 %reduce-scatter.2.cloned.1.call-done = f32[16,3072]{1,0:T(8,128)} async-done(((f32[32,3072]{1,0:T(8,128)}), f32[16,3072]{1,0:T(8,128)}) %reduce-scatter.2.cloned.1.call-update) | async-done | bytes 196624 | tf_op jit(solution)/shard_map/reduce_scatter | solution.py:189
  297.2 1.0 add_convert_fusion
  298.1 0.7 reshape.87
  (98 shorter events, 3.2 us)
Async XLA Ops:
  6.5 53.1 %copy-start = (bf16[192,2,1024]{2,1,0:T(2,128)(2,1)S(1)}, bf16[192,2,1024]{2,1,0:T(2,128)(2,1)}, u32[]{:S(2)}) copy-start(bf16[192,2,1024]{2,1,0:T(2,128)(2,1)} %param.29) | copy-start | bytes 2359300
  6.5 222.4 %all-gather.3.cloned.1.call-start = ((), (), s32[]{:S(2)}) async-start(), calls=%async_computation.1 | async-start | bytes 20054016 | tf_op jit(solution)/shard_map/all_gather | solution.py:157
  7.3 10.0 %copy-start.8 = (s32[512]{0:T(512)S(1)}, s32[512]{0:T(512)}, u32[]{:S(2)}) copy-start(s32[512]{0:T(512)} %param.25) | copy-start | bytes 6148
  7.3 271.6 %all-gather.5.cloned.1.call-start = ((), (), s32[]{:S(2)}) async-start(), calls=%async_computation.2 | async-start | bytes 2228224 | tf_op jit(solution)/shard_map/all_gather | solution.py:183
  17.3 42.4 %copy-start.10 = (f32[2,192]{1,0:T(2,128)S(1)}, f32[2,192]{1,0:T(2,128)}, u32[]{:S(2)}) copy-start(f32[2,192]{1,0:T(2,128)} %param.28) | copy-start | bytes 4612
  59.7 4.0 %copy-start.1 = (bf16[8,2,4,512]{3,2,1,0:T(4,128)(2,1)S(1)}, bf16[8,2,4,512]{3,2,1,0:T(4,128)(2,1)}, u32[]{:S(2)}) copy-start(bf16[8,2,4,512]{3,2,1,0:T(4,128)(2,1)} %param.16) | copy-start | bytes 196612
  69.0 133.1 %copy-start.6 = (f32[512]{0:T(512)S(1)}, f32[512]{0:T(512)}, u32[]{:S(2)}) copy-start(f32[512]{0:T(512)} %param.18) | copy-start | bytes 6148
  69.1 133.1 %copy-start.7 = (f32[512]{0:T(512)S(1)}, f32[512]{0:T(512)}, u32[]{:S(2)}) copy-start(f32[512]{0:T(512)} %param.17) | copy-start | bytes 6148
  69.1 145.4 %copy-start.3 = (f32[3,3072]{1,0:T(4,128)S(1)}, f32[3,3072]{1,0:T(4,128)}, u32[]{:S(2)}) copy-start(f32[3,3072]{1,0:T(4,128)} %param.23) | copy-start | bytes 110596
  202.2 5.1 %collective-permute-start = (bf16[8,1,4,512]{3,0,2,1:T(8,128)(2,1)S(1)}, bf16[8,1,4,512]{3,0,2,1:T(8,128)(2,1)S(1)}, u32[]{:S(2)}, u32[]{:S(2)}) collective-permute-start(bf16[8,1,4,512]{3,0,2,1:T(8,128)(2,1)S(1)} %get-tuple-element.44), channel_id=1, source_target_pairs={{0,2},{2,4},{4,6},{6,8},{8,10},{10,12},{12,14},{14,16},{16,18},{18... | collective-permute-start | bytes 98312 | tf_op jit(solution)/shard_map/ppermute | solution.py:27
  206.0 3.7 %collective-permute-start.1 = (bf16[8,1,4,512]{3,0,2,1:T(8,128)(2,1)S(1)}, bf16[8,1,4,512]{3,0,2,1:T(8,128)(2,1)S(1)}, u32[]{:S(2)}, u32[]{:S(2)}) collective-permute-start(bf16[8,1,4,512]{3,0,2,1:T(8,128)(2,1)S(1)} %get-tuple-element.45), channel_id=1, source_target_pairs={{2,0},{4,2},{6,4},{8,6},{10,8},{12,10},{14,12},{16,14},{18,16},{20... | collective-permute-start | bytes 98312 | tf_op jit(solution)/shard_map/ppermute | solution.py:29
  209.8 5.0 %collective-permute-start.2 = (bf16[8,4,1,512]{3,0,2,1:T(8,128)(2,1)S(1)}, bf16[8,4,1,512]{3,0,2,1:T(8,128)(2,1)S(1)}, u32[]{:S(2)}, u32[]{:S(2)}) collective-permute-start(bf16[8,4,1,512]{3,0,2,1:T(8,128)(2,1)S(1)} %get-tuple-element.42), channel_id=1, source_target_pairs={{0,1},{2,3},{4,5},{6,7},{8,9},{10,11},{12,13},{14,15},{16,17},{18,... | collective-permute-start | bytes 98312 | tf_op jit(solution)/shard_map/ppermute | solution.py:27
  213.2 5.8 %collective-permute-start.3 = (bf16[8,4,1,512]{3,0,2,1:T(8,128)(2,1)S(1)}, bf16[8,4,1,512]{3,0,2,1:T(8,128)(2,1)S(1)}, u32[]{:S(2)}, u32[]{:S(2)}) collective-permute-start(bf16[8,4,1,512]{3,0,2,1:T(8,128)(2,1)S(1)} %get-tuple-element.43), channel_id=1, source_target_pairs={{1,0},{3,2},{5,4},{7,6},{9,8},{11,10},{13,12},{15,14},{17,16},{19,... | collective-permute-start | bytes 98312 | tf_op jit(solution)/shard_map/ppermute | solution.py:29
  219.5 1.0 copy-start.2
  219.5 1.0 copy-start.9
  219.7 1.5 copy-start.4
  239.3 57.8 %reduce-scatter.2.cloned.1.call-start = ((), (), s32[]{:S(2)}) async-start(), calls=%async_computation.3 | async-start | bytes 589824 | tf_op jit(solution)/shard_map/reduce_scatter | solution.py:189
  278.9 4.3 %slice-start = ((s8[6291456]{0:T(1024)(128)(4,1)}), s8[4194304]{0:T(1024)(128)(4,1)S(1)}, s32[]{:S(2)}) async-start(s8[6291456]{0:T(1024)(128)(4,1)} %bitcast.249), calls=%async_computation.4 | async-start | bytes 8388608
  281.2 1.9 slice-start.1
  283.2 14.0 %copy-start.5 = (f32[3072]{0:T(1024)S(1)}, f32[3072]{0:T(1024)}, u32[]{:S(2)}) copy-start(f32[3072]{0:T(1024)} %param.31) | copy-start | bytes 36868
Sparse Core Ops, SparseCore 0:
  8.9 142.0 all-gather.2
  239.4 39.3 all-gather.4
  285.2 11.8 reduce-scatter.1
